TPU v7x, 32 devices: a whole 2x2x4 slice. The times are simulated.
32 devices in a mesh: dom: 32 (over z, y, x, core).
Axes of the slice: x: 2, y: 2, z: 4, core: 2. Of those that a mesh axis runs over, the one named last changes fastest.
Arguments:
- rhs: float32 [128, 12, 512], P('dom'), may hold values from -18 to 18
- stiffness: float32 [512, 512], replicated, may hold values from -0.25 to 0.25
- vol_jac: float32 [128, 12, 12], P('dom'), may hold values from -0.9 to 0.9
- face_jac: float32 [128, 6, 12, 12], P('dom'), may hold values from -1.5 to 1.5
- block_inv: float32 [128, 12, 12, 512], P('dom'), as said below
- face_owner: int32 [128, 6], P('dom'), may hold values from -1 to 31, as said below
- face_elem: int32 [128, 6], P('dom'), may hold values from 0 to 3
- face_side: int32 [128, 6], P('dom'), may hold values from 0 to 5
- face_turn: int32 [128, 6], P('dom'), may hold values from 0 to 7
Outputs:
- correction: float32 [128, 12, 512], P('dom')
Inputs may be any that keep to these rules, and one draw needn't show every extreme that they name: `face_owner`: -1 marks a face with no neighbour; any other value is the element's own partition or one next to it along the axis; of the faces of one partition exactly 8 name the partition below and exactly 8 the partition above, where that partition exists. Each block_inv[e, :, :, m] is a full 12 x 12 matrix.
All inputs are finite; a program needn't handle non-finite values.
Results may differ from a plain program's by a relative error of at most 0.0001.
Values sent between devices are 32-bit elements; how exact they have to be, the bound alone decides.
A program may use at most 64 MiB of HBM per device.

v0:
```python
import jax
import jax.numpy as jnp
import numpy as np
from jax import lax
from jax.sharding import PartitionSpec as P

QF = 8
QC = 4


PRECISE = lax.Precision.HIGHEST
SIGMA = 2.0
OMEGA = 0.7


def from_behind(block, axis, distance):
    devices = range(lax.axis_size(axis))
    route = [(i - distance, i) for i in devices if i - distance in devices]
    return lax.ppermute(block, axis, route)


def trace_table(degree_count, keep_count):
    matrix = np.zeros((degree_count**3, 6 * keep_count * keep_count), np.float32)
    for index_i in range(degree_count):
        for index_j in range(degree_count):
            for index_k in range(degree_count):
                mode_id = (index_i * degree_count + index_j) * degree_count + index_k
                triple = (index_i, index_j, index_k)
                for face_id in range(6):
                    normal_axis = face_id // 2
                    normal = triple[normal_axis]
                    tangent = [triple[place] for place in range(3) if place != normal_axis]
                    if tangent[0] < keep_count and tangent[1] < keep_count:
                        sign_val = (-1.0) ** normal if face_id % 2 == 0 else 1.0
                        column = (
                            face_id * keep_count * keep_count + tangent[0] * keep_count + tangent[1]
                        )
                        matrix[mode_id, column] = sign_val
    return matrix


def lift_table(degree_count):
    matrix = np.zeros((6 * degree_count * degree_count, degree_count**3), np.float32)
    for index_i in range(degree_count):
        for index_j in range(degree_count):
            for index_k in range(degree_count):
                mode_id = (index_i * degree_count + index_j) * degree_count + index_k
                triple = (index_i, index_j, index_k)
                for face_id in range(6):
                    normal_axis = face_id // 2
                    normal = triple[normal_axis]
                    tangent = [triple[place] for place in range(3) if place != normal_axis]
                    sign_val = (-1.0) ** normal if face_id % 2 == 0 else 1.0
                    column = (
                        face_id * degree_count * degree_count
                        + tangent[0] * degree_count
                        + tangent[1]
                    )
                    matrix[column, mode_id] = (2.0 * normal + 1.0) / 16.0 * sign_val
    return matrix


def turn_table(degree_count):
    span = degree_count * degree_count
    matrix = np.zeros((span, 8 * span), np.float32)
    for turn_id in range(8):
        for index_a in range(degree_count):
            for index_b in range(degree_count):
                if turn_id % 2 == 1:
                    source = index_b * degree_count + index_a
                else:
                    source = index_a * degree_count + index_b
                sign_val = 1.0
                if turn_id // 2 % 2 == 1:
                    sign_val = sign_val * (-1.0) ** index_a
                if turn_id // 4 % 2 == 1:
                    sign_val = sign_val * (-1.0) ** index_b
                matrix[source, turn_id * span + index_a * degree_count + index_b] = sign_val
    return matrix


def select_table():
    matrix = np.zeros((QF**3, QC**3), np.float32)
    for index_i in range(QC):
        for index_j in range(QC):
            for index_k in range(QC):
                matrix[
                    (index_i * QF + index_j) * QF + index_k, (index_i * QC + index_j) * QC + index_k
                ] = 1.0
    return matrix


def faces_of(iterate, matrix):
    elements, variables = (iterate.shape[0], iterate.shape[1])
    face_span = matrix.shape[1] // 6
    traced = jnp.dot(iterate.reshape(elements * variables, -1), matrix, precision=PRECISE)
    traced = traced.reshape(elements, variables, 6, face_span).transpose(0, 2, 1, 3)
    return traced.reshape(elements * 6, variables * face_span)


def pick_faces(pooled, slot_ids, turning, present, turns, variables):
    gathered = jnp.take(pooled, slot_ids, axis=0)
    count = gathered.shape[0]
    span = turns.shape[0]
    rotated = jnp.dot(gathered.reshape(count * variables, span), turns, precision=PRECISE)
    rotated = rotated.reshape(count, variables, 8, span)
    weights = (turning[:, None] == jnp.arange(8, dtype=jnp.int32)[None, :]).astype(jnp.float32)
    weights = weights * present.astype(jnp.float32)[:, None]
    oriented = jnp.einsum("cvtq,ct->cvq", rotated, weights, precision=PRECISE)
    return oriented.reshape(count, variables * span)


def finish(iterate, inside, outside, vol_jac, face_jac, kernel, lift):
    elements, variables = (iterate.shape[0], iterate.shape[1])
    face_span = inside.shape[1] // variables
    jump_in = (inside - outside).reshape(elements, 6, variables, face_span)
    jumps = jnp.einsum("efvw,efwq->efvq", face_jac, jump_in, precision=PRECISE)
    lifted = jnp.dot(
        jumps.transpose(0, 2, 1, 3).reshape(elements * variables, 6 * face_span),
        lift,
        precision=PRECISE,
    )
    blended = jnp.dot(iterate.reshape(elements * variables, -1), kernel, precision=PRECISE).reshape(
        elements, variables, -1
    )
    volume = jnp.einsum("evw,ewm->evm", vol_jac, blended, precision=PRECISE)
    return volume + lifted.reshape(elements, variables, -1)


def smooth(inverse, residual):
    summed = inverse[:, :, 0, :] * residual[:, None, 0, :]
    for column in range(1, residual.shape[1]):
        summed = summed + inverse[:, :, column, :] * residual[:, None, column, :]
    return summed


def local(
    rhs, stiffness, vol_jac, face_jac, block_inv, face_owner, face_elem, face_side, face_turn
):
    elements, variables, mode_count = rhs.shape
    me_index = lax.axis_index("dom")
    trace_fine = jnp.asarray(trace_table(QF, QF))
    trace_low = jnp.asarray(trace_table(QF, QC))
    trace_coarse = jnp.asarray(trace_table(QC, QC))
    lift_fine = jnp.asarray(lift_table(QF))
    lift_coarse = jnp.asarray(lift_table(QC))
    turns_fine = jnp.asarray(turn_table(QF))
    turns_coarse = jnp.asarray(turn_table(QC))
    select = jnp.asarray(select_table())

    def restrict(values):
        leading = values.shape[:-1]
        return jnp.dot(values.reshape(-1, values.shape[-1]), select, precision=PRECISE).reshape(
            leading + (select.shape[1],)
        )

    flat_owner = face_owner.reshape(-1)
    flat_slot = (face_elem * 6 + face_side).reshape(-1).astype(jnp.int32)
    present = flat_owner >= 0
    offset = flat_owner - me_index
    slot_full = jnp.where(present, (offset + 1) * (elements * 6) + flat_slot, 0).astype(jnp.int32)
    turning = face_turn.reshape(-1)

    def neighbour_pool(inside):
        shifted = [from_behind(inside, "dom", stride) for stride in (1, -1)]
        return jnp.concatenate([shifted[0], inside, shifted[1]], axis=0)

    def fine_apply(iterate):
        inside = faces_of(iterate, trace_fine)
        outside = pick_faces(
            neighbour_pool(inside), slot_full, turning, present, turns_fine, variables
        )
        return SIGMA * iterate + finish(
            iterate, inside, outside, vol_jac, face_jac, stiffness, lift_fine
        )

    iterate = OMEGA * smooth(block_inv, rhs)
    iterate = iterate + OMEGA * smooth(block_inv, rhs - fine_apply(iterate))
    inside = faces_of(iterate, trace_low)
    shifted = [from_behind(inside, "dom", stride) for stride in (1, -1)]
    pooled = jnp.concatenate([shifted[0], inside, shifted[1]], axis=0)
    outside = pick_faces(pooled, slot_full, turning, present, turns_coarse, variables)
    kernel_low = restrict(stiffness)
    coarse_rhs = restrict(rhs - SIGMA * iterate) - finish(
        iterate, inside, outside, vol_jac, face_jac, kernel_low, lift_coarse
    )
    coarse_inv = restrict(block_inv)
    coarse_mat = restrict(restrict(stiffness).T).T
    sweep_one = OMEGA * smooth(coarse_inv, coarse_rhs)
    inside = faces_of(sweep_one, trace_coarse)
    shifted = [from_behind(inside, "dom", stride) for stride in (1, -1)]
    pooled = jnp.concatenate([shifted[0], inside, shifted[1]], axis=0)
    outside = pick_faces(pooled, slot_full, turning, present, turns_coarse, variables)
    result = SIGMA * sweep_one + finish(
        sweep_one, inside, outside, vol_jac, face_jac, coarse_mat, lift_coarse
    )
    correction_low = sweep_one + OMEGA * smooth(coarse_inv, coarse_rhs - result)
    leading = correction_low.shape[:-1]
    iterate = iterate + jnp.dot(
        correction_low.reshape(-1, correction_low.shape[-1]), select.T, precision=PRECISE
    ).reshape(leading + (select.shape[0],))
    for sweep in range(2):
        iterate = iterate + OMEGA * smooth(block_inv, rhs - fine_apply(iterate))
    return iterate


def solution(mesh):
    return jax.shard_map(
        local,
        mesh=mesh,
        in_specs=(
            P("dom", None, None),
            P(),
            P("dom", None, None),
            P("dom", None, None, None),
            P("dom", None, None, None),
            P("dom", None),
            P("dom", None),
            P("dom", None),
            P("dom", None),
        ),
        out_specs=P("dom", None, None),
        check_vma=False,
    )
```

profile of v0, /device:TPU:23, one launch (start us, length us, event | category | flops | bytes accessed | tf_op | source)
XLA Modules:
  0.0 147.1 jit_solution(13771413384050204893)
XLA Ops:
  0.0 1.8 %fusion.249 = (f32[4,12,1,512]{3,0,2,1:T(4,128)S(1)}, f32[4,12,1,512]{3,0,2,1:T(4,128)S(1)}, f32[4,12,1,512]{3,0,2,1:T(4,128)S(1)}, f32[4,12,1,512]{3,0,2,1:T(4,...) fusion(f32[4,12,12,512]{3,0,2,1:T(4,128)} %param.25), kind=kLoop, calls=%fused_computation.407 | loop fusion | bytes 2359296 | tf_op jit(solution)/shard_map/slice | solution.py:133
  2.0 1.7 %convolution_bitcast_fusion.5 = f32[4,6,12,64]{3,2,1,0:T(8,128)S(1)} fusion(f32[6,64,512,1]{2,1,0,3:T(8,128)S(1)} %copy-done.2, f32[4,12,1,512]{3,0,2,1:T(4,128)S(1)} %get-tuple-element.18, f32[4,12,1,512]{3,0,2,1:T(4,128)S(1)} %get-tuple-element.17, f32[4,12,1,512]{3,0,2,1:T(4,128)S(1)} %get-tuple-element.16, f32[4,12,1,512]{3,0,2,1:T(4,128)S(1)} %get-tuple-element.15, ...), kind=kOutput, calls=%fused_computation.19 | convolution fusion | flops 113836032 | bytes 2138112 | tf_op jit(solution)/shard_map/dot_general | solution.py:96
  3.9 3.7 %collective-permute-start = (f32[24,768]{1,0:T(8,128)S(1)}, f32[24,768]{1,0:T(8,128)S(1)}, u32[]{:S(2)}, u32[]{:S(2)}) collective-permute-start(f32[24,768]{1,0:T(8,128)S(1)} %reshape.370), channel_id=1, source_target_pairs={{0,1},{1,2},{2,3},{3,4},{4,5},{5,6},{6,7},{7,8},{8,9},{9,10},{10,1... | collective-permute-start | bytes 221192 | tf_op jit(solution)/shard_map/ppermute | solution.py:19
  7.5 1.9 %collective-permute-start.1 = (f32[24,768]{1,0:T(8,128)S(1)}, f32[24,768]{1,0:T(8,128)}, u32[]{:S(2)}, u32[]{:S(2)}) collective-permute-start(f32[24,768]{1,0:T(8,128)S(1)} %reshape.370), channel_id=1, source_target_pairs={{1,0},{2,1},{3,2},{4,3},{5,4},{6,5},{7,6},{8,7},{9,8},{10,9},{11,1... | collective-permute-start | bytes 221192 | tf_op jit(solution)/shard_map/ppermute | solution.py:19
  21.5 1.4 fusion.37
  23.0 1.4 fusion.9
  25.5 1.7 %reshape.467 = f32[4,12,384]{2,1,0:T(8,128)} reshape(f32[4,12,6,64]{3,2,1,0:T(8,128)} %copy.834) | data formatting | bytes 147456 | tf_op jit(solution)/shard_map/dot_general | solution.py:118
  27.4 1.9 %fusion.14 = f32[4,12,512]{2,1,0:T(8,128)S(1)} fusion(f32[4,12,512]{2,1,0:T(8,128)} %convolution_bitcast_fusion.10, f32[4,12,384]{2,1,0:T(8,128)} %reshape.467, f32[384,512,1]{1,0,2:T(8,128)S(1)} %copy-done.1, f32[4,12,512]{2,0,1:T(4,128)} %param.21, f32[4,12,512]{2,1,0:T(8,128)} %copy-done.34), kind=kOutput, calls=%fused_computation.28 | convolution fusion | flops 113344512 | bytes 1253376 | tf_op jit(solution)/shard_map/dot_general | solution.py:118
  30.3 2.3 %convolution_bitcast_fusion.6 = f32[4,6,12,16]{3,2,1,0:T(8,128)} fusion(f32[6,16,512,1]{2,1,0,3:T(8,128)S(1)} %copy-done.71, f32[4,12,1,512]{3,0,2,1:T(4,128)S(1)} %copy-done.18, f32[4,12,1,512]{3,0,2,1:T(4,128)S(1)} %copy-done.14, f32[4,12,1,512]{3,0,2,1:T(4,128)S(1)} %copy-done.10, f32[4,12,1,512]{3,0,2,1:T(4,128)S(1)} %copy-done.6, ...), kind=kOutput, calls=%fused_computation.20 | convolution fusion | flops 29515776 | bytes 1591296 | tf_op jit(solution)/shard_map/dot_general | solution.py:96
  32.5 1.6 %reshape.372 = f32[24,192]{1,0:T(8,128)} reshape(f32[4,6,12,16]{3,2,1,0:T(8,128)} %convolution_bitcast_fusion.6) | data formatting | bytes 36864 | tf_op jit(solution)/shard_map/reshape | solution.py:98
  34.2 5.6 %collective-permute-start.2 = (f32[24,192]{1,0:T(8,128)}, f32[24,192]{1,0:T(8,128)S(1)}, u32[]{:S(2)}, u32[]{:S(2)}) collective-permute-start(f32[24,192]{1,0:T(8,128)} %reshape.372), channel_id=1, source_target_pairs={{0,1},{1,2},{2,3},{3,4},{4,5},{5,6},{6,7},{7,8},{8,9},{9,10},{10,1... | collective-permute-start | bytes 55304 | tf_op jit(solution)/shard_map/ppermute | solution.py:19
  39.8 2.1 %collective-permute-start.3 = (f32[24,192]{1,0:T(8,128)}, f32[24,192]{1,0:T(8,128)S(1)}, u32[]{:S(2)}, u32[]{:S(2)}) collective-permute-start(f32[24,192]{1,0:T(8,128)} %reshape.372), channel_id=1, source_target_pairs={{1,0},{2,1},{3,2},{4,3},{5,4},{6,5},{7,6},{8,7},{9,8},{10,9},{11,1... | collective-permute-start | bytes 55304 | tf_op jit(solution)/shard_map/ppermute | solution.py:19
  41.9 1.7 %fusion.115 = f32[4,12,512]{2,1,0:T(8,128)S(1)} fusion(f32[4,12,1,512]{3,0,2,1:T(4,128)} %copy-done.17, f32[4,12,1,512]{3,0,2,1:T(4,128)} %copy-done.13, f32[4,12,1,512]{3,0,2,1:T(4,128)} %copy-done.9, f32[4,12,1,512]{3,0,2,1:T(4,128)} %copy-done.5, f32[4,12,1,512]{3,0,2,1:T(4,128)S(1)} %get-tuple-element.14, f32[4,12,1,512]{3,0,2,1:T(4,128)S(1)} %get-tuple-element.13, ...), kind=kLoop, calls=%fused_computation.178 | loop fusion | flops 638976 | bytes 1474560 | tf_op jit(solution)/shard_map/add | solution.py:178
  47.6 2.2 %gather_fusion.1 = f32[24,192]{1,0:T(8,128)} fusion(f32[72,192]{1,0:T(8,128)} %pad_maximum_fusion.3, s32[1024]{0:T(1024)} %copy-done.130), kind=kCustom, calls=%fused_computation.1.clone | custom fusion | bytes 36960 | tf_op jit(solution)/shard_map/jit(_take)/gather | solution.py:102
  49.8 1.4 broadcast_select_fusion.4
  51.2 1.5 copy.751
  52.7 2.5 %fusion.257 = f32[24,12,8,16]{0,3,2,1:T(8,128)} fusion(f32[24,12,16,1]{0,2,3,1:T(8,128)} %bitcast.655, f32[8,16,16,1]{2,1,0,3:T(8,128)} %constant.92), kind=kOutput, calls=%fused_computation.415 | convolution fusion | flops 7077888 | bytes 174080 | tf_op jit(solution)/shard_map/dot_general | solution.py:105
  55.2 3.0 %copy.816 = f32[24,12,8,16]{3,2,1,0:T(8,128)} copy(f32[24,12,8,16]{0,3,2,1:T(8,128)} %fusion.257) | data formatting | bytes 294912 | tf_op jit(solution)/shard_map/dot_general | solution.py:105
  58.3 2.4 %fusion.258 = f32[24,1,12,16]{3,1,2,0:T(1,128)S(1)} fusion(f32[24,12,8,16]{3,2,1,0:T(8,128)} %copy.816, f32[24,8,1,1]{1,2,3,0:T(1,128)} %bitcast.650), kind=kOutput, calls=%fused_computation.416 | convolution fusion | flops 442368 | bytes 166656 | tf_op jit(solution)/shard_map/cvtq,ct->cvq/dot_general | solution.py:109
  64.3 1.6 %reshape.374 = f32[24,192]{1,0:T(8,128)} reshape(f32[4,6,12,16]{3,2,1,0:T(8,128)} %convolution_bitcast_fusion.7) | data formatting | bytes 36864 | tf_op jit(solution)/shard_map/reshape | solution.py:98
  66.0 4.1 %collective-permute-start.4 = (f32[24,192]{1,0:T(8,128)}, f32[24,192]{1,0:T(8,128)S(1)}, u32[]{:S(2)}, u32[]{:S(2)}) collective-permute-start(f32[24,192]{1,0:T(8,128)} %reshape.374), channel_id=1, source_target_pairs={{0,1},{1,2},{2,3},{3,4},{4,5},{5,6},{6,7},{7,8},{8,9},{9,10},{10,1... | collective-permute-start | bytes 55304 | tf_op jit(solution)/shard_map/ppermute | solution.py:19
  70.1 1.9 %collective-permute-start.5 = (f32[24,192]{1,0:T(8,128)}, f32[24,192]{1,0:T(8,128)S(1)}, u32[]{:S(2)}, u32[]{:S(2)}) collective-permute-start(f32[24,192]{1,0:T(8,128)} %reshape.374), channel_id=1, source_target_pairs={{1,0},{2,1},{3,2},{4,3},{5,4},{6,5},{7,6},{8,7},{9,8},{10,9},{11,1... | collective-permute-start | bytes 55304 | tf_op jit(solution)/shard_map/ppermute | solution.py:19
  74.5 1.5 %convolution_bitcast_fusion.11 = f32[4,12,64]{2,1,0:T(8,128)} fusion(f32[4,12,64]{2,1,0:T(8,128)S(1)} %fusion.224, f32[4,12,12]{2,0,1:T(4,128)} %param.23), kind=kOutput, calls=%fused_computation.38 | convolution fusion | flops 442368 | bytes 26880 | tf_op jit(solution)/shard_map/evw,ewm->evm/dot_general | solution.py:126
  78.6 2.2 %gather_fusion.2 = f32[24,192]{1,0:T(8,128)} fusion(f32[72,192]{1,0:T(8,128)} %pad_maximum_fusion.4, s32[1024]{0:T(1024)} %copy-done.130), kind=kCustom, calls=%fused_computation.4.clone | custom fusion | bytes 36960 | tf_op jit(solution)/shard_map/jit(_take)/gather | solution.py:102
  80.8 1.4 broadcast_select_fusion.3
  82.2 1.5 copy.781
  83.7 2.5 %fusion.259 = f32[24,12,8,16]{0,3,2,1:T(8,128)} fusion(f32[24,12,16,1]{0,2,3,1:T(8,128)} %bitcast.654, f32[8,16,16,1]{2,1,0,3:T(8,128)} %constant.92), kind=kOutput, calls=%fused_computation.417 | convolution fusion | flops 7077888 | bytes 174080 | tf_op jit(solution)/shard_map/dot_general | solution.py:105
  86.2 3.0 %copy.822 = f32[24,12,8,16]{3,2,1,0:T(8,128)} copy(f32[24,12,8,16]{0,3,2,1:T(8,128)} %fusion.259) | data formatting | bytes 294912 | tf_op jit(solution)/shard_map/dot_general | solution.py:105
  89.4 2.6 %fusion.260 = f32[24,1,12,16]{3,1,2,0:T(1,128)S(1)} fusion(f32[24,12,8,16]{3,2,1,0:T(8,128)} %copy.822, f32[24,8,1,1]{1,2,3,0:T(1,128)} %bitcast.651), kind=kOutput, calls=%fused_computation.418 | convolution fusion | flops 442368 | bytes 166656 | tf_op jit(solution)/shard_map/cvtq,ct->cvq/dot_general | solution.py:109
  94.2 2.0 %convolution_bitcast_fusion.3 = f32[4,6,12,64]{3,2,1,0:T(8,128)} fusion(f32[6,64,512,1]{2,1,0,3:T(8,128)S(1)} %copy-done.2, f32[4,12,512]{2,1,0:T(8,128)S(1)} %convolution_add_fusion.3), kind=kOutput, calls=%fused_computation.17 | convolution fusion | flops 113246208 | bytes 958464 | tf_op jit(solution)/shard_map/dot_general | solution.py:96
  96.1 1.6 %reshape.376 = f32[24,768]{1,0:T(8,128)} reshape(f32[4,6,12,64]{3,2,1,0:T(8,128)} %convolution_bitcast_fusion.3) | data formatting | bytes 147456 | tf_op jit(solution)/shard_map/reshape | solution.py:98
  97.8 4.4 %collective-permute-start.6 = (f32[24,768]{1,0:T(8,128)}, f32[24,768]{1,0:T(8,128)S(1)}, u32[]{:S(2)}, u32[]{:S(2)}) collective-permute-start(f32[24,768]{1,0:T(8,128)} %reshape.376), channel_id=1, source_target_pairs={{0,1},{1,2},{2,3},{3,4},{4,5},{5,6},{6,7},{7,8},{8,9},{9,10},{10,1... | collective-permute-start | bytes 221192 | tf_op jit(solution)/shard_map/ppermute | solution.py:19
  102.2 2.1 %collective-permute-start.7 = (f32[24,768]{1,0:T(8,128)}, f32[24,768]{1,0:T(8,128)S(1)}, u32[]{:S(2)}, u32[]{:S(2)}) collective-permute-start(f32[24,768]{1,0:T(8,128)} %reshape.376), channel_id=1, source_target_pairs={{1,0},{2,1},{3,2},{4,3},{5,4},{6,5},{7,6},{8,7},{9,8},{10,9},{11,1... | collective-permute-start | bytes 221192 | tf_op jit(solution)/shard_map/ppermute | solution.py:19
  104.4 1.7 %fusion.22 = f32[4,12,512]{2,1,0:T(8,128)S(1)} fusion(f32[4,12,512]{2,1,0:T(8,128)} %copy-done.26, f32[512,512]{1,0:T(8,128)S(1)} %copy-done), kind=kOutput, calls=%fused_computation.45 | convolution fusion | flops 150994944 | bytes 1245184 | tf_op jit(solution)/shard_map/dot_general | solution.py:123
  106.9 3.0 %collective-permute-done.7 = f32[24,768]{1,0:T(8,128)S(1)} collective-permute-done((f32[24,768]{1,0:T(8,128)}, f32[24,768]{1,0:T(8,128)S(1)}, u32[]{:S(2)}, u32[]{:S(2)}) %collective-permute-start.7) | collective-permute-done | bytes 73760 | tf_op jit(solution)/shard_map/ppermute | solution.py:19
  110.6 2.3 %gather_fusion.3 = f32[24,768]{1,0:T(8,128)} fusion(f32[72,768]{1,0:T(8,128)} %pad_maximum_fusion.1, s32[1024]{0:T(1024)} %copy-done.130), kind=kCustom, calls=%fused_computation.2.clone | custom fusion | bytes 147552 | tf_op jit(solution)/shard_map/jit(_take)/gather | solution.py:102
  112.9 1.6 %broadcast_select_fusion.1 = f32[24,768]{1,0:T(8,128)} fusion(f32[24,768]{1,0:T(8,128)} %gather_fusion.3, pred[24]{0:T(512)(128)(4,1)} %copy-done.128), kind=kLoop, calls=%fused_computation.262 | loop fusion | flops 18432 | bytes 147480 | tf_op jit(solution)/shard_map/jit(_take)/select_n | solution.py:102
  114.5 1.7 %reshape.461 = f32[24,12,64,1]{2,1,0,3:T(8,128)} reshape(f32[24,768]{1,0:T(8,128)} %broadcast_select_fusion.1) | data formatting | bytes 147456 | tf_op jit(solution)/shard_map/dot_general | solution.py:105
  116.1 2.5 %fusion.35 = f32[24,12,8,64]{3,1,2,0:T(8,128)S(1)} fusion(f32[8,64,64,1]{2,1,0,3:T(8,128)} %constant.87, f32[24,12,64,1]{2,1,0,3:T(8,128)} %reshape.461), kind=kOutput, calls=%fused_computation.61 | convolution fusion | flops 113246208 | bytes 794624 | tf_op jit(solution)/shard_map/dot_general | solution.py:105
  121.2 1.6 %reshape.469 = f32[4,12,384]{2,1,0:T(8,128)} reshape(f32[4,12,6,64]{3,2,1,0:T(8,128)} %copy.837) | data formatting | bytes 147456 | tf_op jit(solution)/shard_map/dot_general | solution.py:118
  122.9 1.7 %fusion.15 = f32[4,12,512]{2,1,0:T(8,128)S(1)} fusion(f32[4,12,512]{2,1,0:T(8,128)} %convolution_bitcast_fusion.9, f32[4,12,384]{2,1,0:T(8,128)} %reshape.469, f32[384,512,1]{1,0,2:T(8,128)S(1)} %copy-done.1, f32[4,12,512]{2,0,1:T(4,128)} %param.21, f32[4,12,512]{2,1,0:T(8,128)} %copy-done.26), kind=kOutput, calls=%fused_computation.29 | convolution fusion | flops 113344512 | bytes 1253376 | tf_op jit(solution)/shard_map/dot_general | solution.py:118
  126.0 2.0 %convolution_bitcast_fusion.1 = f32[4,6,12,64]{3,2,1,0:T(8,128)} fusion(f32[6,64,512,1]{2,1,0,3:T(8,128)S(1)} %copy-done.2, f32[4,12,512]{2,1,0:T(8,128)S(1)} %fusion.128), kind=kOutput, calls=%fused_computation.15 | convolution fusion | flops 113246208 | bytes 958464 | tf_op jit(solution)/shard_map/dot_general | solution.py:96
  129.0 2.5 %collective-permute-start.8 = (f32[24,768]{1,0:T(8,128)S(1)}, f32[24,768]{1,0:T(8,128)S(1)}, u32[]{:S(2)}, u32[]{:S(2)}) collective-permute-start(f32[24,768]{1,0:T(8,128)S(1)} %reshape.378), channel_id=1, source_target_pairs={{0,1},{1,2},{2,3},{3,4},{4,5},{5,6},{6,7},{7,8},{8,9},{9,10},{10,1... | collective-permute-start | bytes 221192 | tf_op jit(solution)/shard_map/ppermute | solution.py:19
  131.5 1.9 %collective-permute-start.9 = (f32[24,768]{1,0:T(8,128)S(1)}, f32[24,768]{1,0:T(8,128)S(1)}, u32[]{:S(2)}, u32[]{:S(2)}) collective-permute-start(f32[24,768]{1,0:T(8,128)S(1)} %reshape.378), channel_id=1, source_target_pairs={{1,0},{2,1},{3,2},{4,3},{5,4},{6,5},{7,6},{8,7},{9,8},{10,9},{11,1... | collective-permute-start | bytes 221192 | tf_op jit(solution)/shard_map/ppermute | solution.py:19
  133.4 1.7 %fusion.20 = f32[4,12,512]{2,1,0:T(8,128)S(1)} fusion(f32[4,12,512]{2,1,0:T(8,128)} %copy-done.24, f32[512,512]{1,0:T(8,128)S(1)} %copy-done), kind=kOutput, calls=%fused_computation.43 | convolution fusion | flops 150994944 | bytes 1245184 | tf_op jit(solution)/shard_map/dot_general | solution.py:123
  136.0 2.9 %collective-permute-done.9 = f32[24,768]{1,0:T(8,128)S(1)} collective-permute-done((f32[24,768]{1,0:T(8,128)S(1)}, f32[24,768]{1,0:T(8,128)S(1)}, u32[]{:S(2)}, u32[]{:S(2)}) %collective-permute-start.9) | collective-permute-done | bytes 73760 | tf_op jit(solution)/shard_map/ppermute | solution.py:19
  139.9 1.4 fusion.33
  141.3 1.4 fusion.5
  (381 shorter events, 40.6 us)
Async XLA Ops:
  0.0 10.5 %copy-start = (f32[512,512]{1,0:T(8,128)S(1)}, f32[512,512]{1,0:T(8,128)}, u32[]{:S(2)}) copy-start(f32[512,512]{1,0:T(8,128)} %param.22) | copy-start | bytes 3145732
  1.8 7.9 %copy-start.5 = (f32[4,12,1,512]{3,0,2,1:T(4,128)}, f32[4,12,1,512]{3,0,2,1:T(4,128)S(1)}, u32[]{:S(2)}) copy-start(f32[4,12,1,512]{3,0,2,1:T(4,128)S(1)} %get-tuple-element.15) | copy-start | bytes 294916
  1.8 7.9 %copy-start.9 = (f32[4,12,1,512]{3,0,2,1:T(4,128)}, f32[4,12,1,512]{3,0,2,1:T(4,128)S(1)}, u32[]{:S(2)}) copy-start(f32[4,12,1,512]{3,0,2,1:T(4,128)S(1)} %get-tuple-element.16) | copy-start | bytes 294916
  1.8 7.9 %copy-start.13 = (f32[4,12,1,512]{3,0,2,1:T(4,128)}, f32[4,12,1,512]{3,0,2,1:T(4,128)S(1)}, u32[]{:S(2)}) copy-start(f32[4,12,1,512]{3,0,2,1:T(4,128)S(1)} %get-tuple-element.17) | copy-start | bytes 294916
  1.8 7.9 %copy-start.17 = (f32[4,12,1,512]{3,0,2,1:T(4,128)}, f32[4,12,1,512]{3,0,2,1:T(4,128)S(1)}, u32[]{:S(2)}) copy-start(f32[4,12,1,512]{3,0,2,1:T(4,128)S(1)} %get-tuple-element.18) | copy-start | bytes 294916
  1.9 7.8 %copy-start.78 = (f32[4,512]{1,0:T(4,128)}, f32[4,512]{1,0:T(4,128)S(1)}, u32[]{:S(2)}) copy-start(f32[4,512]{1,0:T(4,128)S(1)} %get-tuple-element.67) | copy-start | bytes 24580
  1.9 7.8 %copy-start.80 = (f32[4,512]{1,0:T(4,128)}, f32[4,512]{1,0:T(4,128)S(1)}, u32[]{:S(2)}) copy-start(f32[4,512]{1,0:T(4,128)S(1)} %get-tuple-element.68) | copy-start | bytes 24580
  1.9 7.8 %copy-start.82 = (f32[4,512]{1,0:T(4,128)}, f32[4,512]{1,0:T(4,128)S(1)}, u32[]{:S(2)}) copy-start(f32[4,512]{1,0:T(4,128)S(1)} %get-tuple-element.69) | copy-start | bytes 24580
  1.9 7.8 %copy-start.84 = (f32[4,512]{1,0:T(4,128)}, f32[4,512]{1,0:T(4,128)S(1)}, u32[]{:S(2)}) copy-start(f32[4,512]{1,0:T(4,128)S(1)} %get-tuple-element.70) | copy-start | bytes 24580
  1.9 7.8 %copy-start.86 = (f32[4,512]{1,0:T(4,128)}, f32[4,512]{1,0:T(4,128)S(1)}, u32[]{:S(2)}) copy-start(f32[4,512]{1,0:T(4,128)S(1)} %get-tuple-element.71) | copy-start | bytes 24580
  1.9 7.8 %copy-start.88 = (f32[4,512]{1,0:T(4,128)}, f32[4,512]{1,0:T(4,128)S(1)}, u32[]{:S(2)}) copy-start(f32[4,512]{1,0:T(4,128)S(1)} %get-tuple-element.72) | copy-start | bytes 24580
  1.9 7.8 %copy-start.90 = (f32[4,512]{1,0:T(4,128)}, f32[4,512]{1,0:T(4,128)S(1)}, u32[]{:S(2)}) copy-start(f32[4,512]{1,0:T(4,128)S(1)} %get-tuple-element.73) | copy-start | bytes 24580
  1.9 7.8 %copy-start.92 = (f32[4,512]{1,0:T(4,128)}, f32[4,512]{1,0:T(4,128)S(1)}, u32[]{:S(2)}) copy-start(f32[4,512]{1,0:T(4,128)S(1)} %get-tuple-element.74) | copy-start | bytes 24580
  1.9 7.8 %copy-start.94 = (f32[4,512]{1,0:T(4,128)}, f32[4,512]{1,0:T(4,128)S(1)}, u32[]{:S(2)}) copy-start(f32[4,512]{1,0:T(4,128)S(1)} %get-tuple-element.75) | copy-start | bytes 24580
  2.0 7.8 %copy-start.96 = (f32[4,512]{1,0:T(4,128)}, f32[4,512]{1,0:T(4,128)S(1)}, u32[]{:S(2)}) copy-start(f32[4,512]{1,0:T(4,128)S(1)} %get-tuple-element.76) | copy-start | bytes 24580
  2.0 7.8 %copy-start.98 = (f32[4,512]{1,0:T(4,128)}, f32[4,512]{1,0:T(4,128)S(1)}, u32[]{:S(2)}) copy-start(f32[4,512]{1,0:T(4,128)S(1)} %get-tuple-element.77) | copy-start | bytes 24580
  2.0 7.8 %copy-start.100 = (f32[4,512]{1,0:T(4,128)}, f32[4,512]{1,0:T(4,128)S(1)}, u32[]{:S(2)}) copy-start(f32[4,512]{1,0:T(4,128)S(1)} %get-tuple-element.78) | copy-start | bytes 24580
  2.0 7.5 %copy-start.131 = (s32[4,6]{1,0:T(4,128)S(1)}, s32[4,6]{1,0:T(4,128)}, u32[]{:S(2)}) copy-start(s32[4,6]{1,0:T(4,128)} %param.26) | copy-start | bytes 292
  2.0 7.5 %copy-start.132 = (s32[4,6]{1,0:T(4,128)S(1)}, s32[4,6]{1,0:T(4,128)}, u32[]{:S(2)}) copy-start(s32[4,6]{1,0:T(4,128)} %param.28) | copy-start | bytes 292
  2.0 7.5 %copy-start.133 = (s32[4,6]{1,0:T(4,128)S(1)}, s32[4,6]{1,0:T(4,128)}, u32[]{:S(2)}) copy-start(s32[4,6]{1,0:T(4,128)} %param.27) | copy-start | bytes 292
  3.8 5.9 %copy-start.39 = (f32[4,6,12,64]{3,2,1,0:T(8,128)}, f32[4,6,12,64]{3,2,1,0:T(8,128)S(1)}, u32[]{:S(2)}) copy-start(f32[4,6,12,64]{3,2,1,0:T(8,128)S(1)} %convolution_bitcast_fusion.5) | copy-start | bytes 221188
  3.8 6.6 %copy-start.134 = (s32[4,6]{1,0:T(4,128)S(1)}, s32[4,6]{1,0:T(4,128)}, u32[]{:S(2)}) copy-start(s32[4,6]{1,0:T(4,128)} %param.29) | copy-start | bytes 292
  3.9 15.9 %collective-permute-start = (f32[24,768]{1,0:T(8,128)S(1)}, f32[24,768]{1,0:T(8,128)S(1)}, u32[]{:S(2)}, u32[]{:S(2)}) collective-permute-start(f32[24,768]{1,0:T(8,128)S(1)} %reshape.370), channel_id=1, source_target_pairs={{0,1},{1,2},{2,3},{3,4},{4,5},{5,6},{6,7},{7,8},{8,9},{9,10},{10,1... | collective-permute-start | bytes 221192 | tf_op jit(solution)/shard_map/ppermute | solution.py:19
  7.5 12.2 %collective-permute-start.1 = (f32[24,768]{1,0:T(8,128)S(1)}, f32[24,768]{1,0:T(8,128)}, u32[]{:S(2)}, u32[]{:S(2)}) collective-permute-start(f32[24,768]{1,0:T(8,128)S(1)} %reshape.370), channel_id=1, source_target_pairs={{1,0},{2,1},{3,2},{4,3},{5,4},{6,5},{7,6},{8,7},{9,8},{10,9},{11,1... | collective-permute-start | bytes 221192 | tf_op jit(solution)/shard_map/ppermute | solution.py:19
  9.6 11.7 %copy-start.128 = (pred[24]{0:T(512)(128)(4,1)}, pred[24]{0:T(512)(128)(4,1)S(1)}, u32[]{:S(2)}) copy-start(pred[24]{0:T(512)(128)(4,1)S(1)} %compare_and_fusion) | copy-start | bytes 76
  13.8 5.9 %copy-start.28 = (f32[4,12,12,64]{3,2,1,0:T(8,128)}, f32[4,12,12,64]{3,2,1,0:T(8,128)S(1)}, u32[]{:S(2)}) copy-start(f32[4,12,12,64]{3,2,1,0:T(8,128)S(1)} %fusion.2) | copy-start | bytes 442372
  15.0 7.9 %copy-start.53 = (f32[24,8]{1,0:T(8,128)}, f32[24,8]{1,0:T(8,128)S(1)}, u32[]{:S(2)}) copy-start(f32[24,8]{1,0:T(8,128)S(1)} %fusion.240) | copy-start | bytes 2308
  15.0 6.5 %copy-start.30 = (f32[8,64,64,1]{2,1,0,3:T(8,128)S(1)}, f32[8,64,64,1]{2,1,0,3:T(8,128)}, u32[]{:S(2)}) copy-start(f32[8,64,64,1]{2,1,0,3:T(8,128)} %constant.87) | copy-start | bytes 393220
  34.2 9.4 %copy-start.42 = (f32[64,512]{1,0:T(8,128)S(1)}, f32[64,512]{1,0:T(8,128)}, u32[]{:S(2)}) copy-start(f32[64,512]{1,0:T(8,128)} %copy-done.41) | copy-start | bytes 393220
  34.2 9.7 %copy-start.22 = (f32[4,12,512]{2,0,1:T(4,128)S(1)}, f32[4,12,512]{2,0,1:T(4,128)}, u32[]{:S(2)}) copy-start(f32[4,12,512]{2,0,1:T(4,128)} %param.21) | copy-start | bytes 294916
  34.2 9.7 %copy-start.47 = (f32[512,64,1]{0,1,2:T(8,128)S(1)}, f32[512,64,1]{0,1,2:T(8,128)}, u32[]{:S(2)}) copy-start(f32[512,64,1]{0,1,2:T(8,128)} %constant.90) | copy-start | bytes 393220
  34.2 10.6 %copy-start.44 = (f32[4,12,12]{2,0,1:T(4,128)S(1)}, f32[4,12,12]{2,0,1:T(4,128)}, u32[]{:S(2)}) copy-start(f32[4,12,12]{2,0,1:T(4,128)} %param.23) | copy-start | bytes 6916
  34.2 12.7 %copy-start.102 = (f32[24,192]{1,0:T(8,128)S(1)}, f32[24,192]{1,0:T(8,128)}, u32[]{:S(2)}) copy-start(f32[24,192]{1,0:T(8,128)} %reshape.372) | copy-start | bytes 55300
  34.2 11.4 %collective-permute-start.2 = (f32[24,192]{1,0:T(8,128)}, f32[24,192]{1,0:T(8,128)S(1)}, u32[]{:S(2)}, u32[]{:S(2)}) collective-permute-start(f32[24,192]{1,0:T(8,128)} %reshape.372), channel_id=1, source_target_pairs={{0,1},{1,2},{2,3},{3,4},{4,5},{5,6},{6,7},{7,8},{8,9},{9,10},{10,1... | collective-permute-start | bytes 55304 | tf_op jit(solution)/shard_map/ppermute | solution.py:19
  39.8 7.2 %collective-permute-start.3 = (f32[24,192]{1,0:T(8,128)}, f32[24,192]{1,0:T(8,128)S(1)}, u32[]{:S(2)}, u32[]{:S(2)}) collective-permute-start(f32[24,192]{1,0:T(8,128)} %reshape.372), channel_id=1, source_target_pairs={{1,0},{2,1},{3,2},{4,3},{5,4},{6,5},{7,6},{8,7},{9,8},{10,9},{11,1... | collective-permute-start | bytes 55304 | tf_op jit(solution)/shard_map/ppermute | solution.py:19
  58.2 4.3 %copy-start.29 = (f32[4,12,12,64]{3,2,1,0:T(8,128)S(1)}, f32[4,12,12,64]{3,2,1,0:T(8,128)}, u32[]{:S(2)}) copy-start(f32[4,12,12,64]{3,2,1,0:T(8,128)} %copy-done.28) | copy-start | bytes 442372
  66.0 10.1 %collective-permute-start.4 = (f32[24,192]{1,0:T(8,128)}, f32[24,192]{1,0:T(8,128)S(1)}, u32[]{:S(2)}, u32[]{:S(2)}) collective-permute-start(f32[24,192]{1,0:T(8,128)} %reshape.374), channel_id=1, source_target_pairs={{0,1},{1,2},{2,3},{3,4},{4,5},{5,6},{6,7},{7,8},{8,9},{9,10},{10,1... | collective-permute-start | bytes 55304 | tf_op jit(solution)/shard_map/ppermute | solution.py:19
  70.1 7.2 %collective-permute-start.5 = (f32[24,192]{1,0:T(8,128)}, f32[24,192]{1,0:T(8,128)S(1)}, u32[]{:S(2)}, u32[]{:S(2)}) collective-permute-start(f32[24,192]{1,0:T(8,128)} %reshape.374), channel_id=1, source_target_pairs={{1,0},{2,1},{3,2},{4,3},{5,4},{6,5},{7,6},{8,7},{9,8},{10,9},{11,1... | collective-permute-start | bytes 55304 | tf_op jit(solution)/shard_map/ppermute | solution.py:19
  89.3 3.8 %copy-start.33 = (f32[4,12,512]{2,1,0:T(8,128)S(1)}, f32[4,12,512]{2,1,0:T(8,128)}, u32[]{:S(2)}) copy-start(f32[4,12,512]{2,1,0:T(8,128)} %copy-done.32) | copy-start | bytes 294916
  97.8 8.2 %copy-start.45 = (f32[4,12,12]{2,0,1:T(4,128)S(1)}, f32[4,12,12]{2,0,1:T(4,128)}, u32[]{:S(2)}) copy-start(f32[4,12,12]{2,0,1:T(4,128)} %param.23) | copy-start | bytes 6916
  97.8 12.1 %copy-start.56 = (f32[24,768]{1,0:T(8,128)S(1)}, f32[24,768]{1,0:T(8,128)}, u32[]{:S(2)}) copy-start(f32[24,768]{1,0:T(8,128)} %reshape.376) | copy-start | bytes 221188
  97.8 9.1 %collective-permute-start.6 = (f32[24,768]{1,0:T(8,128)}, f32[24,768]{1,0:T(8,128)S(1)}, u32[]{:S(2)}, u32[]{:S(2)}) collective-permute-start(f32[24,768]{1,0:T(8,128)} %reshape.376), channel_id=1, source_target_pairs={{0,1},{1,2},{2,3},{3,4},{4,5},{5,6},{6,7},{7,8},{8,9},{9,10},{10,1... | collective-permute-start | bytes 221192 | tf_op jit(solution)/shard_map/ppermute | solution.py:19
  102.2 7.7 %collective-permute-start.7 = (f32[24,768]{1,0:T(8,128)}, f32[24,768]{1,0:T(8,128)S(1)}, u32[]{:S(2)}, u32[]{:S(2)}) collective-permute-start(f32[24,768]{1,0:T(8,128)} %reshape.376), channel_id=1, source_target_pairs={{1,0},{2,1},{3,2},{4,3},{5,4},{6,5},{7,6},{8,7},{9,8},{10,9},{11,1... | collective-permute-start | bytes 221192 | tf_op jit(solution)/shard_map/ppermute | solution.py:19
  127.9 7.1 %copy-start.46 = (f32[4,12,12]{2,0,1:T(4,128)S(1)}, f32[4,12,12]{2,0,1:T(4,128)}, u32[]{:S(2)}) copy-start(f32[4,12,12]{2,0,1:T(4,128)} %param.23) | copy-start | bytes 6916
  129.0 10.7 %copy-start.129 = (pred[24]{0:T(512)(128)(4,1)S(1)}, pred[24]{0:T(512)(128)(4,1)}, u32[]{:S(2)}) copy-start(pred[24]{0:T(512)(128)(4,1)} %copy-done.128) | copy-start | bytes 76
  129.0 7.0 %collective-permute-start.8 = (f32[24,768]{1,0:T(8,128)S(1)}, f32[24,768]{1,0:T(8,128)S(1)}, u32[]{:S(2)}, u32[]{:S(2)}) collective-permute-start(f32[24,768]{1,0:T(8,128)S(1)} %reshape.378), channel_id=1, source_target_pairs={{0,1},{1,2},{2,3},{3,4},{4,5},{5,6},{6,7},{7,8},{8,9},{9,10},{10,1... | collective-permute-start | bytes 221192 | tf_op jit(solution)/shard_map/ppermute | solution.py:19
  131.5 7.5 %collective-permute-start.9 = (f32[24,768]{1,0:T(8,128)S(1)}, f32[24,768]{1,0:T(8,128)S(1)}, u32[]{:S(2)}, u32[]{:S(2)}) collective-permute-start(f32[24,768]{1,0:T(8,128)S(1)} %reshape.378), channel_id=1, source_target_pairs={{1,0},{2,1},{3,2},{4,3},{5,4},{6,5},{7,6},{8,7},{9,8},{10,9},{11,1... | collective-permute-start | bytes 221192 | tf_op jit(solution)/shard_map/ppermute | solution.py:19
  135.1 4.8 %copy-start.31 = (f32[8,64,64,1]{2,1,0,3:T(8,128)S(1)}, f32[8,64,64,1]{2,1,0,3:T(8,128)}, u32[]{:S(2)}) copy-start(f32[8,64,64,1]{2,1,0,3:T(8,128)} %constant.87) | copy-start | bytes 393220
  (97 other events, 202.6 us)
where the time goes:
time: 149 us; the launch traced here: 147 us
  matrix products  50.8 us (34%)
  local copies, waits for them, and re-layouts  42.5 us (29%)
  starting transfers between devices  30.2 us (20%)
  other arithmetic  12.7 us (9%)
  waiting for transfers between devices  8.44 us (6%)
  between operations  2.32 us (2%)
    ppermute x10, starting transfers between devices, from_behind(): return lax.ppermute(block, axis, route)  30.2 us
    dot_general x5, matrix products, pick_faces(): jnp.dot(gathered.reshape(count * variables, span), turns, precision=PRECISE)  10.3 us
    dot_general x5, matrix products, pick_faces(): oriented = jnp.einsum('cvtq,ct->cvq', rotated, weights, precision=PRECISE)  9.23 us
    dot_general x5, matrix products, faces_of(): jnp.dot(iterate.reshape(elements * variables, -1), matrix, precision=PREC...  9.2 us
    ppermute x10, waiting for transfers between devices, from_behind(): return lax.ppermute(block, axis, route)  8.44 us
    gather x5, local copies, waits for them, and re-layouts, pick_faces(): gathered = jnp.take(pooled, slot_ids, axis=0)  8.02 us
    dot_general x5, local copies, waits for them, and re-layouts, pick_faces(): jnp.dot(gathered.reshape(count * variables, span), turns, precision=PRECISE)  7.94 us
    dot_general x6, local copies, waits for them, and re-layouts, finish(): jnp.dot(jumps.transpose(0, 2, 1, 3).reshape(elements * variables, 6 * fac...  6.55 us
  transfers between devices with their start and end apart: 10, of which 4 were waited for; matrix products, arithmetic and copies ran while one was open for 15% of the time, Pallas kernels for 0%

commit v1 on v0

v1 whole, which is shorter than its diff:
```python
import functools

import jax
import jax.numpy as jnp
import numpy as np
from jax import lax
from jax.experimental import pallas as pl
from jax.experimental.pallas import tpu as pltpu
from jax.sharding import PartitionSpec as P

QF = 8
QC = 4
SIGMA = 2.0
OMEGA = 0.7
SPAN = QF * QF
STEPS = 5
MESH = pl.DeviceIdType.MESH


def split_index(mode_id):
    return (mode_id // (QF * QF), mode_id // QF % QF, mode_id % QF)


def trace_table():
    matrix = np.zeros((QF**3, 6 * 2 * SPAN), np.float32)
    for mode_id in range(QF**3):
        triple = split_index(mode_id)
        for face_id in range(6):
            axis = face_id // 2
            a, b = [triple[place] for place in range(3) if place != axis]
            sign = (-1.0) ** triple[axis] if face_id % 2 == 0 else 1.0
            plain, turned = a * QF + b, b * QF + a
            low, high = (plain, turned) if face_id % 2 == 0 else (turned, plain)
            matrix[mode_id, face_id * 2 * SPAN + low] = sign
            matrix[mode_id, face_id * 2 * SPAN + SPAN + high] = sign
    return matrix


def lift_table():
    matrix = np.zeros((6 * SPAN, QF**3), np.float32)
    for mode_id in range(QF**3):
        triple = split_index(mode_id)
        for face_id in range(6):
            axis = face_id // 2
            a, b = [triple[place] for place in range(3) if place != axis]
            sign = (-1.0) ** triple[axis] if face_id % 2 == 0 else 1.0
            matrix[face_id * SPAN + a * QF + b, mode_id] = (2.0 * triple[axis] + 1.0) / 16.0 * sign
    return matrix


def sign_table():
    matrix = np.zeros((17, 16, 2 * SPAN), np.float32)
    for odd in range(2):
        for turn in range(8):
            half = (turn % 2) ^ odd
            for a in range(QF):
                for b in range(QF):
                    sign = 1.0
                    if turn // 2 % 2 == 1:
                        sign *= (-1.0) ** a
                    if turn // 4 % 2 == 1:
                        sign *= (-1.0) ** b
                    matrix[turn + 8 * odd, :, half * SPAN + a * QF + b] = sign
    return matrix


def low_mask():
    mask = np.zeros((8, QF**3), np.float32)
    for mode_id in range(QF**3):
        if max(split_index(mode_id)) < QC:
            mask[:, mode_id] = 1.0
    return mask


def halves(value):
    high = value.astype(jnp.bfloat16)
    return high, (value - high.astype(jnp.float32)).astype(jnp.bfloat16)


def kernel(
    n, elements, variables,
    owner, elem, side_of, turn, rhs, vol, face, signs, mask, inv_hbm, trace_hbm, stiff_hbm, lift_hbm,
    out,
    inv, inv_raw, trace, stiff, lift, stiff_hi, stiff_lo, jac_wide, vol_wide, small, jump, table,
    meta, request, asked, asked_s, base_ref, now_ref, work_ref, kept_ref, coarse_ref, fine_ref,
    sent, got0, got1, got2, got3, got4,
    load_sem, ask_send, ask_recv, ask_local, send_sem, recv_sem,
):
    got = (got0, got1, got2, got3, got4)
    me = lax.axis_index("dom")
    has = (me > 0, me < n - 1)
    other = (jnp.maximum(me - 1, 0), jnp.minimum(me + 1, n - 1))
    modes = rhs.shape[2]
    rows = elements * variables
    pairs = rows // 8
    half_reach = elements

    loads = []
    for at, (source, target) in enumerate(
        ((inv_hbm, inv_raw), (trace_hbm, trace), (stiff_hbm, stiff), (lift_hbm, lift))
    ):
        loads.append(pltpu.make_async_copy(source, target, load_sem.at[at]))
        loads[-1].start()

    barrier = pltpu.get_barrier_semaphore()
    for side in range(2):
        @pl.when(has[side])
        def _():
            pl.semaphore_signal(barrier, inc=1, device_id=(other[side],), device_id_type=MESH)

    spots = lax.broadcasted_iota(jnp.int32, (1, 128), 1)
    wanted = [jnp.zeros((1, 128), jnp.int32), jnp.zeros((1, 128), jnp.int32)]
    ranks = [jnp.int32(0), jnp.int32(0)]
    for e in range(elements):
        for f in range(6):
            at = e * 6 + f
            home = owner[e, f]
            face_turn, face_side, face_elem = turn[e, f], side_of[e, f], elem[e, f]
            present = home >= 0
            odd = face_side % 2
            swap = face_turn % 2
            half = (odd + swap) % 2
            tests = (present & (home == me - 1), present & (home == me + 1))
            for side in range(2):
                value = (face_elem * 6 + face_side) * 2 + half
                wanted[side] = jnp.where((spots == ranks[side]) & tests[side], value, wanted[side])
            rank = jnp.where(tests[1], ranks[1], ranks[0])
            far = tests[0] | tests[1]
            far_half = rank // half_reach
            meta[0, at] = jnp.where(tests[1], 1, 0)
            meta[1, at] = jnp.minimum(rank % half_reach, half_reach - 1)
            meta[2, at] = jnp.where(far, 1, 0)
            sign_row = face_turn + 8 * jnp.where(far, (far_half + swap) % 2, odd)
            meta[3, at] = jnp.where(present, sign_row, 16)
            for side in range(2):
                ranks[side] = ranks[side] + jnp.where(tests[side], 1, 0)
    request[0:1, :] = wanted[0]
    request[1:2, :] = wanted[1]

    pl.semaphore_wait(barrier, jnp.where(me > 0, 1, 0) + jnp.where(me < n - 1, 1, 0))

    def ask(side, slot):
        return pltpu.make_async_remote_copy(
            src_ref=request, dst_ref=asked.at[slot], send_sem=ask_send.at[side],
            recv_sem=ask_recv.at[slot], device_id=(other[side],), device_id_type=MESH,
        )

    for side in range(2):
        @pl.when(has[side])
        def _():
            ask(side, 1 - side).start()

    def twice(ref, w, lanes):
        row = ref[elements * w : elements * (w + 1), lanes]
        return jnp.concatenate([row, row], axis=0)

    def contract(wide, wide_lanes, source, c):
        lanes = slice(c * 128, (c + 1) * 128)
        totals = [None] * pairs
        for w in range(variables):
            row = twice(source, w, lanes)
            for p in range(pairs):
                term = wide[w, 8 * p : 8 * p + 8, wide_lanes] * row
                totals[p] = term if totals[p] is None else totals[p] + term
        return totals

    def smooth(source, width, emit):
        for c in range(width // 128):
            lanes = slice(c * 128, (c + 1) * 128)
            for p, total in enumerate(contract(inv, lanes, source, c)):
                emit(slice(8 * p, 8 * p + 8), lanes, OMEGA * total)

    for v in range(variables):
        base_ref[elements * v : elements * (v + 1), :] = rhs[v]
    loads[0].wait()
    for v in range(variables):
        for w in range(variables):
            inv[w, elements * v : elements * (v + 1), :] = inv_raw[v, w]

    def first(at, lanes, value):
        now_ref[at, lanes] = value

    def following(at, lanes, value):
        now_ref[at, lanes] = now_ref[at, lanes] + value

    smooth(base_ref, modes, first)

    for side in range(2):
        @pl.when(has[side])
        def _():
            ask(side, side).wait()
            copy = pltpu.make_async_copy(asked.at[side], asked_s.at[side], ask_local.at[side])
            copy.start()
            copy.wait()

    lane = lax.broadcasted_iota(jnp.int32, (variables, 2 * SPAN), 1)
    in_low = lane < SPAN

    def put(step, side, slot):
        return pltpu.make_async_remote_copy(
            src_ref=sent.at[step, side], dst_ref=got[step].at[slot], send_sem=send_sem.at[step, side],
            recv_sem=recv_sem.at[step, slot], device_id=(other[side],), device_id_type=MESH,
        )

    def face_load(place):
        return table[place % 6, pl.ds(place // 6, variables, stride=elements), :]

    def widen_jacobians():
        for f in range(6):
            for v in range(variables):
                small[f, elements * v : elements * (v + 1), :] = face[f, v]
        for v in range(variables):
            small[6, elements * v : elements * (v + 1), :] = vol[v]
        low8 = lax.broadcasted_iota(jnp.int32, (rows, 2 * SPAN), 1) < SPAN
        for w in range(variables):
            vol_wide[w] = jnp.broadcast_to(small[6, :, w : w + 1], (rows, 2 * SPAN))
            for pair in range(3):
                one = jnp.broadcast_to(small[2 * pair, :, w : w + 1], (rows, 2 * SPAN))
                two = jnp.broadcast_to(small[2 * pair + 1, :, w : w + 1], (rows, 2 * SPAN))
                jac_wide[w, :, pair * 2 * SPAN : (pair + 1) * 2 * SPAN] = jnp.where(low8, one, two)

    def residual(step, base, width_in, width_out, emit):
        value = now_ref[:, :width_in]
        high, low = halves(value)
        both = jnp.concatenate([high, low], axis=0)
        if step == 0:
            loads[1].wait()
        traced = jnp.dot(both, trace[:width_in, :], preferred_element_type=jnp.float32)
        traced = traced[:rows] + traced[rows:]
        for f in range(6):
            table[f] = traced[:, f * 2 * SPAN : (f + 1) * 2 * SPAN]
        for side in range(2):
            @pl.when(has[side])
            def _():
                for j in range(half_reach):
                    found = []
                    for half in range(2):
                        code = jnp.clip(asked_s[side, 1 - side, half * half_reach + j], 0, 12 * elements - 1)
                        piece = face_load(code // 2)
                        found.append(jnp.where(code % 2 == half, piece, pltpu.roll(piece, SPAN, axis=1)))
                    sent[step, side, j] = jnp.where(in_low, found[0], found[1])
                put(step, side, 1 - side).start()
        if step == 0:
            loads[2].wait()
            stiff_high, stiff_low = halves(stiff[...])
            stiff_hi[...] = stiff_high
            stiff_lo[...] = stiff_low
            widen_jacobians()
        blended = jnp.dot(both, stiff_hi[:width_in, :width_out], preferred_element_type=jnp.float32)
        blended = blended[:rows] + blended[rows:]
        blended = blended + jnp.dot(high, stiff_lo[:width_in, :width_out], preferred_element_type=jnp.float32)
        work_ref[:, :width_out] = blended
        for c in range(width_out // 128):
            lanes = slice(c * 128, (c + 1) * 128)
            for p, total in enumerate(contract(vol_wide, slice(0, 128), work_ref, c)):
                at = slice(8 * p, 8 * p + 8)
                kept_ref[at, lanes] = base[at, lanes] - SIGMA * now_ref[at, lanes] - total
        for side in range(2):
            @pl.when(has[side])
            def _():
                put(step, side, side).wait()
        if step == 0:
            loads[3].wait()
        for e in range(elements):
            for pair in range(3):
                faces = []
                for f in (2 * pair, 2 * pair + 1):
                    at = e * 6 + f
                    own = face_load(elem[e, f] * 6 + side_of[e, f])
                    far = got[step][meta[0, at], meta[1, at]]
                    picked = jnp.where(meta[2, at] > 0, far, own)
                    picked = picked * signs[meta[3, at]][:variables]
                    faces.append(picked + pltpu.roll(picked, SPAN, axis=1))
                at_e = pl.ds(e, variables, stride=elements)
                mine = jnp.where(in_low, table[2 * pair, at_e, :], table[2 * pair + 1, at_e, :])
                theirs = jnp.where(in_low, faces[0], faces[1])
                jump[pair, at_e, :] = mine - theirs
        columns = []
        for pair in range(3):
            lanes = slice(pair * 128, (pair + 1) * 128)
            columns.append(jnp.concatenate(contract(jac_wide, lanes, jump.at[pair], 0), axis=0))
        flux_high, flux_low = halves(jnp.concatenate(columns, axis=1))
        lifted = jnp.dot(
            jnp.concatenate([flux_high, flux_low], axis=0), lift[:, :width_out],
            preferred_element_type=jnp.float32,
        )
        emit(kept_ref[:, :width_out] - (lifted[:rows] + lifted[rows:]))

    short = QC * SPAN
    low_of = jnp.concatenate([mask[:, :short]] * pairs, axis=0)

    def to_work(value):
        work_ref[...] = value

    def to_coarse(value):
        coarse_ref[:, :short] = value * low_of

    def to_low_work(value):
        work_ref[:, :short] = value * low_of

    residual(0, base_ref, modes, modes, to_work)
    smooth(work_ref, modes, following)
    residual(1, base_ref, modes, short, to_coarse)
    fine_ref[...] = now_ref[...]
    smooth(coarse_ref, short, first)
    residual(2, coarse_ref, short, short, to_low_work)
    smooth(work_ref, short, following)
    now_ref[:, :short] = now_ref[:, :short] + fine_ref[:, :short]
    for step in (3, 4):
        residual(step, base_ref, modes, modes, to_work)
        smooth(work_ref, modes, following)
    for v in range(variables):
        out[v] = now_ref[elements * v : elements * (v + 1), :]


def local(n, rhs, stiffness, vol_jac, face_jac, block_inv, face_owner, face_elem, face_side, face_turn):
    elements, variables, modes = rhs.shape
    reach = 2 * elements
    trace = jnp.asarray(trace_table(), jnp.bfloat16)
    lift = jnp.asarray(lift_table(), jnp.bfloat16)
    rows = elements * variables
    vmem = pl.BlockSpec(memory_space=pltpu.VMEM)
    smem = pl.BlockSpec(memory_space=pltpu.SMEM)
    hbm = pl.BlockSpec(memory_space=pl.ANY)
    f32, bf16, i32 = jnp.float32, jnp.bfloat16, jnp.int32
    dma = pltpu.SemaphoreType.DMA
    state = pltpu.VMEM((rows, modes), f32)
    result = pl.pallas_call(
        functools.partial(kernel, n, elements, variables),
        out_shape=jax.ShapeDtypeStruct((variables, elements, modes), f32),
        in_specs=[smem] * 4 + [vmem] * 5 + [hbm] * 4,
        out_specs=vmem,
        scratch_shapes=[
            pltpu.VMEM((variables, rows, modes), f32),
            pltpu.VMEM((variables, variables, elements, modes), f32),
            pltpu.VMEM(trace.shape, bf16),
            pltpu.VMEM(stiffness.shape, f32),
            pltpu.VMEM(lift.shape, bf16),
            pltpu.VMEM(stiffness.shape, bf16),
            pltpu.VMEM(stiffness.shape, bf16),
            pltpu.VMEM((variables, rows, 6 * SPAN), f32),
            pltpu.VMEM((variables, rows, 2 * SPAN), f32),
            pltpu.VMEM((7, rows, variables), f32),
            pltpu.VMEM((3, rows, 2 * SPAN), f32),
            pltpu.VMEM((6, rows, 2 * SPAN), f32),
            pltpu.SMEM((4, 6 * elements), i32),
            pltpu.VMEM((8, 128), i32),
            pltpu.VMEM((2, 8, 128), i32),
            pltpu.SMEM((2, 8, 128), i32),
            state, state, state, state, state, state,
            pltpu.VMEM((STEPS, 2, elements, variables, 2 * SPAN), f32),
        ] + [pltpu.VMEM((2, elements, variables, 2 * SPAN), f32)] * STEPS + [
            dma((4,)),
            dma((2,)),
            dma((2,)),
            dma((2,)),
            dma((STEPS, 2)),
            dma((STEPS, 2)),
        ],
        compiler_params=pltpu.CompilerParams(
            collective_id=0, has_side_effects=True, vmem_limit_bytes=60 * 1024 * 1024
        ),
    )(
        face_owner, face_elem, face_side, face_turn,
        rhs.transpose(1, 0, 2), vol_jac.transpose(1, 0, 2), face_jac.transpose(1, 2, 0, 3),
        jnp.asarray(sign_table()), jnp.asarray(low_mask()),
        block_inv.transpose(1, 2, 0, 3), trace, stiffness, lift,
    )
    return result.transpose(1, 0, 2)


def solution(mesh):
    return jax.shard_map(
        functools.partial(local, mesh.shape["dom"]),
        mesh=mesh,
        in_specs=(
            P("dom", None, None),
            P(),
            P("dom", None, None),
            P("dom", None, None, None),
            P("dom", None, None, None),
            P("dom", None),
            P("dom", None),
            P("dom", None),
            P("dom", None),
        ),
        out_specs=P("dom", None, None),
        check_vma=False,
    )
```

time: 149 us -> 31.3 us (0.21); the launches traced: 147 us -> 31.2 us
  matrix products: 50.8 us -> 0 us
  local copies, waits for them, and re-layouts: 42.5 us -> 1.54 us
  starting transfers between devices: 30.2 us -> 0 us
  Pallas kernels: 0 us -> 29.6 us
  other arithmetic: 12.7 us -> 0 us
  waiting for transfers between devices: 8.44 us -> 0 us
  between operations: 2.32 us -> 0.01 us
    dot_general x40 -> x0, matrix products: 50.8 us -> none  [the longest x5 10.3 us: pick_faces(): jnp.dot(gathered.reshape(count * variables, span), turns, precision=PRECISE)]
    ppermute x10 -> x0, starting transfers between devices: 30.2 us -> none  [from_behind(): return lax.ppermute(block, axis, route)]
    pallas_call x0 -> x1, Pallas kernels: none -> 29.6 us  [local(): pl.pallas_call(functools.partial(kernel, n, elements, variables), out_sha...]
    dot_general x16 -> x0, local copies, waits for them, and re-layouts: 14.6 us -> none  [the longest x5 7.94 us: pick_faces(): jnp.dot(gathered.reshape(count * variables, span), turns, precision=PRECISE)]
    ppermute x10 -> x0, waiting for transfers between devices: 8.44 us -> none  [from_behind(): return lax.ppermute(block, axis, route)]
    gather x5 -> x0, local copies, waits for them, and re-layouts: 8.02 us -> none  [pick_faces(): gathered = jnp.take(pooled, slot_ids, axis=0)]
    reshape x5 -> x0, local copies, waits for them, and re-layouts: 6.05 us -> none  [faces_of(): return traced.reshape(elements * 6, variables * face_span)]
    select_n x7 -> x0, other arithmetic: 4.6 us -> none  [the longest x6 4.59 us: pick_faces(): gathered = jnp.take(pooled, slot_ids, axis=0)]
  transfers between devices with their start and end apart: 10 -> 0, of which waited for: 4 -> 0; matrix products, arithmetic and copies ran while one was open for 15% -> 0% of each run, Pallas kernels for 0% -> 0%
where the time goes in v1:
time: 31.3 us; the launch traced here: 31.2 us
  Pallas kernels  29.6 us (95%)
  local copies, waits for them, and re-layouts  1.54 us (5%)
    pallas_call x1, Pallas kernels, local(): pl.pallas_call(functools.partial(kernel, n, elements, variables), out_sha...  29.6 us
    unnamed x1, local copies, waits for them, and re-layouts  1.54 us

profile of v1, /device:TPU:23, one launch (start us, length us, event | category | flops | bytes accessed | tf_op | source)
XLA Modules:
  0.0 31.2 jit_solution(714931041748539542)
XLA Ops:
  0.0 29.6 %shard_map.127 = f32[12,4,512]{2,1,0:T(4,128)} custom-call(s32[4,6]{1,0:T(4,128)} %owner.1, s32[4,6]{1,0:T(4,128)} %elem.1, s32[4,6]{1,0:T(4,128)} %side_of.1, s32[4,6]{1,0:T(4,128)} %turn.1, f32[12,4,512]{2,1,0:T(4,128)} %bitcast.8, f32[12,4,12]{2,1,0:T(4,128)} %bitcast.9, f32[6,12,4,12]{3,2,1,0:T(4,128)} %bitcast.7, f32[17,16,128]{2,1,0:T(8,128)} %constant.10.clone.signs, ...), custom_call_target="tpu_custom_call" | custom-call | tf_op jit(solution)/shard_map/pallas_call | solution.py:328
  29.6 1.5 %copy.15 = f32[4,12,512]{2,0,1:T(4,128)} copy(f32[4,12,512]{2,0,1:T(4,128)} %bitcast.6) | data formatting | bytes 196608

commit v2 on v1

--- a/solution.py
+++ b/solution.py
@@ -79,34 +79,42 @@
 
 def kernel(
     n, elements, variables,
-    owner, elem, side_of, turn, rhs, vol, face, signs, mask, inv_hbm, trace_hbm, stiff_hbm, lift_hbm,
+    owner_hbm, elem_hbm, side_hbm, turn_hbm, rhs_hbm, vol_hbm, face_hbm, signs_hbm, mask_hbm,
+    inv_hbm, trace_hbm, stiff_hbm, lift_hbm,
     out,
+    owner, elem, side_of, turn, rhs, vol, face, signs, mask,
     inv, inv_raw, trace, stiff, lift, stiff_hi, stiff_lo, jac_wide, vol_wide, small, jump, table,
-    meta, request, asked, asked_s, base_ref, now_ref, work_ref, kept_ref, coarse_ref, fine_ref,
+    meta, request, asked_s, base_ref, now_ref, work_ref, kept_ref, coarse_ref, fine_ref,
     sent, got0, got1, got2, got3, got4,
-    load_sem, ask_send, ask_recv, ask_local, send_sem, recv_sem,
+    load_sem, ask_send, ask_recv, send_sem, recv_sem,
 ):
     got = (got0, got1, got2, got3, got4)
     me = lax.axis_index("dom")
     has = (me > 0, me < n - 1)
     other = (jnp.maximum(me - 1, 0), jnp.minimum(me + 1, n - 1))
-    modes = rhs.shape[2]
+    modes = rhs_hbm.shape[2]
     rows = elements * variables
     pairs = rows // 8
     half_reach = elements
-
-    loads = []
-    for at, (source, target) in enumerate(
-        ((inv_hbm, inv_raw), (trace_hbm, trace), (stiff_hbm, stiff), (lift_hbm, lift))
-    ):
-        loads.append(pltpu.make_async_copy(source, target, load_sem.at[at]))
-        loads[-1].start()
 
     barrier = pltpu.get_barrier_semaphore()
     for side in range(2):
         @pl.when(has[side])
         def _():
             pl.semaphore_signal(barrier, inc=1, device_id=(other[side],), device_id_type=MESH)
+
+    loads = {}
+    for at, (name, source, target) in enumerate((
+        ("owner", owner_hbm, owner), ("elem", elem_hbm, elem), ("side", side_hbm, side_of),
+        ("turn", turn_hbm, turn), ("rhs", rhs_hbm, rhs), ("inv", inv_hbm, inv_raw),
+        ("trace", trace_hbm, trace), ("stiff", stiff_hbm, stiff), ("vol", vol_hbm, vol),
+        ("face", face_hbm, face), ("signs", signs_hbm, signs), ("mask", mask_hbm, mask),
+        ("lift", lift_hbm, lift),
+    )):
+        loads[name] = pltpu.make_async_copy(source, target, load_sem.at[at])
+        loads[name].start()
+    for name in ("owner", "elem", "side", "turn"):
+        loads[name].wait()
 
     spots = lax.broadcasted_iota(jnp.int32, (1, 128), 1)
     wanted = [jnp.zeros((1, 128), jnp.int32), jnp.zeros((1, 128), jnp.int32)]
@@ -141,7 +149,7 @@
 
     def ask(side, slot):
         return pltpu.make_async_remote_copy(
-            src_ref=request, dst_ref=asked.at[slot], send_sem=ask_send.at[side],
+            src_ref=request, dst_ref=asked_s.at[slot], send_sem=ask_send.at[side],
             recv_sem=ask_recv.at[slot], device_id=(other[side],), device_id_type=MESH,
         )
 
@@ -170,9 +178,10 @@
             for p, total in enumerate(contract(inv, lanes, source, c)):
                 emit(slice(8 * p, 8 * p + 8), lanes, OMEGA * total)
 
+    loads["rhs"].wait()
     for v in range(variables):
         base_ref[elements * v : elements * (v + 1), :] = rhs[v]
-    loads[0].wait()
+    loads["inv"].wait()
     for v in range(variables):
         for w in range(variables):
             inv[w, elements * v : elements * (v + 1), :] = inv_raw[v, w]
@@ -189,9 +198,6 @@
         @pl.when(has[side])
         def _():
             ask(side, side).wait()
-            copy = pltpu.make_async_copy(asked.at[side], asked_s.at[side], ask_local.at[side])
-            copy.start()
-            copy.wait()
 
     lane = lax.broadcasted_iota(jnp.int32, (variables, 2 * SPAN), 1)
     in_low = lane < SPAN
@@ -224,7 +230,7 @@
         high, low = halves(value)
         both = jnp.concatenate([high, low], axis=0)
         if step == 0:
-            loads[1].wait()
+            loads["trace"].wait()
         traced = jnp.dot(both, trace[:width_in, :], preferred_element_type=jnp.float32)
         traced = traced[:rows] + traced[rows:]
         for f in range(6):
@@ -241,10 +247,12 @@
                     sent[step, side, j] = jnp.where(in_low, found[0], found[1])
                 put(step, side, 1 - side).start()
         if step == 0:
-            loads[2].wait()
+            loads["stiff"].wait()
             stiff_high, stiff_low = halves(stiff[...])
             stiff_hi[...] = stiff_high
             stiff_lo[...] = stiff_low
+            loads["vol"].wait()
+            loads["face"].wait()
             widen_jacobians()
         blended = jnp.dot(both, stiff_hi[:width_in, :width_out], preferred_element_type=jnp.float32)
         blended = blended[:rows] + blended[rows:]
@@ -260,7 +268,8 @@
             def _():
                 put(step, side, side).wait()
         if step == 0:
-            loads[3].wait()
+            loads["lift"].wait()
+            loads["signs"].wait()
         for e in range(elements):
             for pair in range(3):
                 faces = []
@@ -287,6 +296,7 @@
         emit(kept_ref[:, :width_out] - (lifted[:rows] + lifted[rows:]))
 
     short = QC * SPAN
+    loads["mask"].wait()
     low_of = jnp.concatenate([mask[:, :short]] * pairs, axis=0)
 
     def to_work(value):
@@ -318,19 +328,28 @@
     reach = 2 * elements
     trace = jnp.asarray(trace_table(), jnp.bfloat16)
     lift = jnp.asarray(lift_table(), jnp.bfloat16)
+    signs, mask = jnp.asarray(sign_table()), jnp.asarray(low_mask())
     rows = elements * variables
     vmem = pl.BlockSpec(memory_space=pltpu.VMEM)
-    smem = pl.BlockSpec(memory_space=pltpu.SMEM)
-    hbm = pl.BlockSpec(memory_space=pl.ANY)
+    hbm = pl.BlockSpec(memory_space=pltpu.HBM)
     f32, bf16, i32 = jnp.float32, jnp.bfloat16, jnp.int32
     dma = pltpu.SemaphoreType.DMA
     state = pltpu.VMEM((rows, modes), f32)
     result = pl.pallas_call(
         functools.partial(kernel, n, elements, variables),
         out_shape=jax.ShapeDtypeStruct((variables, elements, modes), f32),
-        in_specs=[smem] * 4 + [vmem] * 5 + [hbm] * 4,
+        in_specs=[hbm] * 13,
         out_specs=vmem,
         scratch_shapes=[
+            pltpu.SMEM(face_owner.shape, i32),
+            pltpu.SMEM(face_owner.shape, i32),
+            pltpu.SMEM(face_owner.shape, i32),
+            pltpu.SMEM(face_owner.shape, i32),
+            pltpu.VMEM((variables, elements, modes), f32),
+            pltpu.VMEM((variables, elements, variables), f32),
+            pltpu.VMEM((6, variables, elements, variables), f32),
+            pltpu.VMEM(signs.shape, f32),
+            pltpu.VMEM(mask.shape, f32),
             pltpu.VMEM((variables, rows, modes), f32),
             pltpu.VMEM((variables, variables, elements, modes), f32),
             pltpu.VMEM(trace.shape, bf16),
@@ -345,13 +364,11 @@
             pltpu.VMEM((6, rows, 2 * SPAN), f32),
             pltpu.SMEM((4, 6 * elements), i32),
             pltpu.VMEM((8, 128), i32),
-            pltpu.VMEM((2, 8, 128), i32),
             pltpu.SMEM((2, 8, 128), i32),
             state, state, state, state, state, state,
             pltpu.VMEM((STEPS, 2, elements, variables, 2 * SPAN), f32),
         ] + [pltpu.VMEM((2, elements, variables, 2 * SPAN), f32)] * STEPS + [
-            dma((4,)),
-            dma((2,)),
+            dma((13,)),
             dma((2,)),
             dma((2,)),
             dma((STEPS, 2)),
@@ -363,7 +380,7 @@
     )(
         face_owner, face_elem, face_side, face_turn,
         rhs.transpose(1, 0, 2), vol_jac.transpose(1, 0, 2), face_jac.transpose(1, 2, 0, 3),
-        jnp.asarray(sign_table()), jnp.asarray(low_mask()),
+        signs, mask,
         block_inv.transpose(1, 2, 0, 3), trace, stiffness, lift,
     )
     return result.transpose(1, 0, 2)

time: 31.3 us -> 29.3 us (0.936)
  Pallas kernels: 29.6 us -> 27.6 us
    pallas_call x1, Pallas kernels: 29.6 us -> 27.6 us  [local(): pl.pallas_call(functools.partial(kernel, n, elements, variables), out_sha...]
where the time goes in v2:
time: 29.3 us; the launch traced here: 29.2 us
  Pallas kernels  27.6 us (94%)
  local copies, waits for them, and re-layouts  1.54 us (5%)
    pallas_call x1, Pallas kernels, local(): pl.pallas_call(functools.partial(kernel, n, elements, variables), out_sha...  27.6 us
    unnamed x1, local copies, waits for them, and re-layouts  1.54 us

profile of v2, /device:TPU:23, one launch (start us, length us, event | category | flops | bytes accessed | tf_op | source)
XLA Modules:
  0.0 29.2 jit_solution(14611113121760589760)
XLA Ops:
  0.0 27.6 %shard_map.127 = f32[12,4,512]{2,1,0:T(4,128)} custom-call(s32[4,6]{1,0:T(4,128)} %owner_hbm.1, s32[4,6]{1,0:T(4,128)} %elem_hbm.1, s32[4,6]{1,0:T(4,128)} %side_hbm.1, s32[4,6]{1,0:T(4,128)} %turn_hbm.1, f32[12,4,512]{2,1,0:T(4,128)} %bitcast.8, f32[12,4,12]{2,1,0:T(4,128)} %bitcast.9, f32[6,12,4,12]{3,2,1,0:T(4,128)} %bitcast.7, ...), custom_call_target="tpu_custom_call" | custom-call | tf_op jit(solution)/shard_map/pallas_call | solution.py:338
  27.6 1.5 %copy.15 = f32[4,12,512]{2,0,1:T(4,128)} copy(f32[4,12,512]{2,0,1:T(4,128)} %bitcast.6) | data formatting | bytes 196608

commit v3 on v2

--- a/solution.py
+++ b/solution.py
@@ -83,7 +83,7 @@
     inv_hbm, trace_hbm, stiff_hbm, lift_hbm,
     out,
     owner, elem, side_of, turn, rhs, vol, face, signs, mask,
-    inv, inv_raw, trace, stiff, lift, stiff_hi, stiff_lo, jac_wide, vol_wide, small, jump, table,
+    inv, inv_raw, trace, stiff, lift, stiff_hi, stiff_lo, jac_wide, vol_wide, small, jump, table, whole,
     meta, request, asked_s, base_ref, now_ref, work_ref, kept_ref, coarse_ref, fine_ref,
     sent, got0, got1, got2, got3, got4,
     load_sem, ask_send, ask_recv, send_sem, recv_sem,
@@ -140,6 +140,7 @@
             meta[2, at] = jnp.where(far, 1, 0)
             sign_row = face_turn + 8 * jnp.where(far, (far_half + swap) % 2, odd)
             meta[3, at] = jnp.where(present, sign_row, 16)
+            meta[4, at] = jnp.where(present, face_turn + 8 * odd, 16)
             for side in range(2):
                 ranks[side] = ranks[side] + jnp.where(tests[side], 1, 0)
     request[0:1, :] = wanted[0]
@@ -194,21 +195,17 @@
 
     smooth(base_ref, modes, first)
 
-    for side in range(2):
-        @pl.when(has[side])
-        def _():
-            ask(side, side).wait()
 
     lane = lax.broadcasted_iota(jnp.int32, (variables, 2 * SPAN), 1)
     in_low = lane < SPAN
 
     def put(step, side, slot):
         return pltpu.make_async_remote_copy(
-            src_ref=sent.at[step, side], dst_ref=got[step].at[slot], send_sem=send_sem.at[step, side],
+            src_ref=whole if step == 0 else sent.at[step - 1, side], dst_ref=got[step].at[slot], send_sem=send_sem.at[step, side],
             recv_sem=recv_sem.at[step, slot], device_id=(other[side],), device_id_type=MESH,
         )
 
-    def face_load(place):
+    def face_load(table, place):
         return table[place % 6, pl.ds(place // 6, variables, stride=elements), :]
 
     def widen_jacobians():
@@ -229,22 +226,25 @@
         value = now_ref[:, :width_in]
         high, low = halves(value)
         both = jnp.concatenate([high, low], axis=0)
+        tab = whole if step == 0 else table
         if step == 0:
             loads["trace"].wait()
         traced = jnp.dot(both, trace[:width_in, :], preferred_element_type=jnp.float32)
         traced = traced[:rows] + traced[rows:]
         for f in range(6):
-            table[f] = traced[:, f * 2 * SPAN : (f + 1) * 2 * SPAN]
+            tab[f] = traced[:, f * 2 * SPAN : (f + 1) * 2 * SPAN]
         for side in range(2):
             @pl.when(has[side])
             def _():
-                for j in range(half_reach):
+                if step == 1:
+                    ask(side, side).wait()
+                for j in range(half_reach if step else 0):
                     found = []
                     for half in range(2):
                         code = jnp.clip(asked_s[side, 1 - side, half * half_reach + j], 0, 12 * elements - 1)
-                        piece = face_load(code // 2)
+                        piece = face_load(tab, code // 2)
                         found.append(jnp.where(code % 2 == half, piece, pltpu.roll(piece, SPAN, axis=1)))
-                    sent[step, side, j] = jnp.where(in_low, found[0], found[1])
+                    sent[step - 1, side, j] = jnp.where(in_low, found[0], found[1])
                 put(step, side, 1 - side).start()
         if step == 0:
             loads["stiff"].wait()
@@ -275,13 +275,17 @@
                 faces = []
                 for f in (2 * pair, 2 * pair + 1):
                     at = e * 6 + f
-                    own = face_load(elem[e, f] * 6 + side_of[e, f])
-                    far = got[step][meta[0, at], meta[1, at]]
+                    place = elem[e, f] * 6 + side_of[e, f]
+                    own = face_load(tab, place)
+                    if step == 0:
+                        far = face_load(got[0].at[meta[0, at]], place)
+                    else:
+                        far = got[step][meta[0, at], meta[1, at]]
                     picked = jnp.where(meta[2, at] > 0, far, own)
-                    picked = picked * signs[meta[3, at]][:variables]
+                    picked = picked * signs[meta[4 if step == 0 else 3, at]][:variables]
                     faces.append(picked + pltpu.roll(picked, SPAN, axis=1))
                 at_e = pl.ds(e, variables, stride=elements)
-                mine = jnp.where(in_low, table[2 * pair, at_e, :], table[2 * pair + 1, at_e, :])
+                mine = jnp.where(in_low, tab[2 * pair, at_e, :], tab[2 * pair + 1, at_e, :])
                 theirs = jnp.where(in_low, faces[0], faces[1])
                 jump[pair, at_e, :] = mine - theirs
         columns = []
@@ -362,12 +366,14 @@
             pltpu.VMEM((7, rows, variables), f32),
             pltpu.VMEM((3, rows, 2 * SPAN), f32),
             pltpu.VMEM((6, rows, 2 * SPAN), f32),
-            pltpu.SMEM((4, 6 * elements), i32),
+            pltpu.VMEM((6, rows, 2 * SPAN), f32),
+            pltpu.SMEM((5, 6 * elements), i32),
             pltpu.VMEM((8, 128), i32),
             pltpu.SMEM((2, 8, 128), i32),
             state, state, state, state, state, state,
-            pltpu.VMEM((STEPS, 2, elements, variables, 2 * SPAN), f32),
-        ] + [pltpu.VMEM((2, elements, variables, 2 * SPAN), f32)] * STEPS + [
+            pltpu.VMEM((STEPS - 1, 2, elements, variables, 2 * SPAN), f32),
+            pltpu.VMEM((2, 6, rows, 2 * SPAN), f32),
+        ] + [pltpu.VMEM((2, elements, variables, 2 * SPAN), f32)] * (STEPS - 1) + [
             dma((13,)),
             dma((2,)),
             dma((2,)),
@@ -375,14 +381,13 @@
             dma((STEPS, 2)),
         ],
         compiler_params=pltpu.CompilerParams(
-            collective_id=0, has_side_effects=True, vmem_limit_bytes=60 * 1024 * 1024
+            collective_id=0, has_side_effects=True, vmem_limit_bytes=40 * 1024 * 1024
         ),
-    )(
+    )(*[pltpu.with_memory_space_constraint(operand, pltpu.HBM) for operand in (
         face_owner, face_elem, face_side, face_turn,
         rhs.transpose(1, 0, 2), vol_jac.transpose(1, 0, 2), face_jac.transpose(1, 2, 0, 3),
-        signs, mask,
-        block_inv.transpose(1, 2, 0, 3), trace, stiffness, lift,
-    )
+        signs, mask, block_inv.transpose(1, 2, 0, 3), trace, stiffness, lift,
+    )])
     return result.transpose(1, 0, 2)
 
 

time: 29.3 us -> 26.2 us (0.89)
  Pallas kernels: 27.6 us -> 25.3 us
  local copies, waits for them, and re-layouts: 1.54 us -> 0.64 us
    pallas_call x1, Pallas kernels: 27.6 us -> 25.3 us  [local(): pl.pallas_call(functools.partial(kernel, n, elements, variables), out_sha...]
    unnamed x1, local copies, waits for them, and re-layouts: 1.54 us -> 0.64 us
where the time goes in v3:
time: 26.2 us; the launch traced here: 25.9 us
  Pallas kernels  25.3 us (97%)
  local copies, waits for them, and re-layouts  0.64 us (2%)
    pallas_call x1, Pallas kernels, local(): pl.pallas_call(functools.partial(kernel, n, elements, variables), out_sha...  25.3 us
    unnamed x1, local copies, waits for them, and re-layouts  0.64 us

profile of v3, /device:TPU:23, one launch (start us, length us, event | category | flops | bytes accessed | tf_op | source)
XLA Modules:
  0.0 25.9 jit_solution(1530268303623026765)
XLA Ops:
  0.0 25.3 %shard_map.127 = f32[12,4,512]{2,1,0:T(4,128)S(1)} custom-call(s32[4,6]{1,0:T(4,128)} %owner_hbm.1, s32[4,6]{1,0:T(4,128)} %elem_hbm.1, s32[4,6]{1,0:T(4,128)} %side_hbm.1, s32[4,6]{1,0:T(4,128)} %turn_hbm.1, f32[12,4,512]{2,1,0:T(4,128)} %bitcast.8, f32[12,4,12]{2,1,0:T(4,128)} %bitcast.9, f32[6,12,4,12]{3,2,1,0:T(4,128)} %bitcast.7, ...), custom_call_target="tpu_custom_call" | custom-call | tf_op jit(solution)/shard_map/pallas_call | solution.py:342
  25.3 0.6 %copy.15 = f32[4,12,512]{2,0,1:T(4,128)} copy(f32[4,12,512]{2,0,1:T(4,128)S(1)} %bitcast.5) | data formatting | bytes 196608
